TPU v7x, 32 devices: a whole 2x2x4 slice. The times are simulated.
32 devices in a mesh: dp: 8 (over y, x, core), seq: 4 (over z).
Axes of the slice: x: 2, y: 2, z: 4, core: 2. Of those that a mesh axis runs over, the one named last changes fastest.
Arguments:
- queries: bfloat16 [4096, 4096], P(('dp', 'seq')), may hold values from -300 to 300
- key_proj: bfloat16 [4096, 512], P(('dp', 'seq')), may hold values from -4.5 to 4.5
- value_proj: bfloat16 [4096, 512], P(('dp', 'seq')), may hold values from -6 to 6
- seq_lengths: int32 [32], replicated, may hold values from 1 to 257, 4096 in all
Outputs:
- attended: bfloat16 [4096, 4096], P(('dp', 'seq'))
Inputs may be any that keep to these rules, and one draw needn't show every extreme that they name: `seq_lengths`: the sequences cover all 4096 tokens; the longest has exactly 257 tokens.
All inputs are finite; a program needn't handle non-finite values.
Results may differ from a plain program's by a relative error of at most 0.0036.
Values may be sent and summed in bfloat16 or wider, within the bound.
No kernel may reach another device: no remote copies, remote signals or barrier semaphores. Data moves between devices by JAX's collectives and lax.ppermute only.
A program may use at most 64 MiB of HBM per device.

v0:
```python
import math
import jax
import jax.numpy as jnp
from jax import lax
from jax.sharding import PartitionSpec as P

HD = 128
QH = 32
KVH = 4
score_scale = 0.08838834764831845
neg_fill = -1e30


def from_behind(block, axis, distance):
    devices = range(lax.axis_size(axis))
    route = [(i - distance, i) for i in devices if i - distance in devices]
    return lax.ppermute(block, axis, route)


def segment_starts(seq_lengths, positions):
    seq_ends = jnp.cumsum(seq_lengths)
    begins = seq_ends - seq_lengths
    covered = begins[None, :] <= positions[:, None]
    return jnp.max(jnp.where(covered, begins[None, :], 0), axis=1)


def attend(
    queries,
    own_keys,
    own_values,
    tail_keys,
    tail_values,
    query_pos,
    key_pos,
    tail_pos,
    query_start,
    tail_limit,
):
    row_count = queries.shape[0]
    heads_query = queries.shape[1]
    group_size = heads_query // own_keys.shape[1]
    tile_rows = math.gcd(row_count, 512)
    tail_count = tail_keys.shape[0]
    pieces = []
    for offset in range(0, row_count, tile_rows):
        query_tile = queries[offset : offset + tile_rows]
        pos_tile = query_pos[offset : offset + tile_rows]
        start_tile = query_start[offset : offset + tile_rows]
        key_count = offset + tile_rows
        keys_used = own_keys[:key_count]
        values_used = own_values[:key_count]
        pos_used = key_pos[:key_count]
        own_mask = (pos_used[None, :] <= pos_tile[:, None]) & (
            pos_used[None, :] >= start_tile[:, None]
        )
        use_tail = offset < tail_limit
        tail_mask = tail_pos[None, :] >= start_tile[:, None]
        reached = jnp.any(tail_mask)

        def one_head(head_index):
            shared_index = head_index // group_size
            query_head = lax.dynamic_index_in_dim(query_tile, head_index, 1, keepdims=False)
            key_head = lax.dynamic_index_in_dim(keys_used, shared_index, 1, keepdims=False)
            value_head = lax.dynamic_index_in_dim(values_used, shared_index, 1, keepdims=False)
            own_scores = (
                jnp.einsum("qd,kd->qk", query_head, key_head, preferred_element_type=jnp.float32)
                * score_scale
            )
            own_scores = jnp.where(own_mask, own_scores, neg_fill)
            row_max = jnp.max(own_scores, axis=1)
            if use_tail:
                tail_key = lax.dynamic_index_in_dim(tail_keys, shared_index, 1, keepdims=False)
                tail_value = lax.dynamic_index_in_dim(tail_values, shared_index, 1, keepdims=False)

                def tail_scores_fn():
                    raw = (
                        jnp.einsum(
                            "qd,kd->qk", query_head, tail_key, preferred_element_type=jnp.float32
                        )
                        * score_scale
                    )
                    return jnp.where(tail_mask, raw, neg_fill)

                def tail_empty():
                    return jnp.full((tile_rows, tail_count), neg_fill, jnp.float32)

                tail_scores = lax.cond(reached, tail_scores_fn, tail_empty)
                row_max = jnp.maximum(row_max, jnp.max(tail_scores, axis=1))
            own_weights = jnp.where(own_mask, jnp.exp(own_scores - row_max[:, None]), 0.0)
            row_sum = jnp.sum(own_weights, axis=1)
            weighted = jnp.dot(
                own_weights.astype(jnp.bfloat16), value_head, preferred_element_type=jnp.float32
            )
            if use_tail:
                tail_weights = jnp.where(tail_mask, jnp.exp(tail_scores - row_max[:, None]), 0.0)
                row_sum = row_sum + jnp.sum(tail_weights, axis=1)

                def tail_product():
                    return jnp.dot(
                        tail_weights.astype(jnp.bfloat16),
                        tail_value,
                        preferred_element_type=jnp.float32,
                    )

                def tail_zero():
                    return jnp.zeros((tile_rows, value_head.shape[1]), jnp.float32)

                weighted = weighted + lax.cond(reached, tail_product, tail_zero)
            return (weighted / row_sum[:, None]).astype(jnp.bfloat16)

        per_head = lax.map(one_head, jnp.arange(heads_query, dtype=jnp.int32))
        pieces.append(jnp.transpose(per_head, (1, 0, 2)))
    return jnp.concatenate(pieces, axis=0)


def body(queries, key_proj, value_proj, seq_lengths):
    tok_rows = queries.shape[0]
    members = lax.axis_size("seq")
    home_index = lax.axis_index("dp")
    block_rows = tok_rows * members
    reach_rows = block_rows // 2
    block_start = home_index * block_rows
    key_pos = block_start + jnp.arange(block_rows, dtype=jnp.int32)
    tail_pos = block_start - reach_rows + jnp.arange(reach_rows, dtype=jnp.int32)
    local_heads = QH // members
    copies = max(1, members // KVH)
    query_split = queries.reshape(tok_rows, members, local_heads * HD)
    key_split = key_proj.reshape(tok_rows, KVH, HD)
    value_split = value_proj.reshape(tok_rows, KVH, HD)
    if copies > 1:
        key_split = jnp.repeat(key_split, copies, axis=1)
        value_split = jnp.repeat(value_split, copies, axis=1)
    query_block, key_block, value_block = (
        lax.all_to_all(query_split, "seq", split_axis=1, concat_axis=0, tiled=True),
        lax.all_to_all(key_split, "seq", split_axis=1, concat_axis=0, tiled=True),
        lax.all_to_all(value_split, "seq", split_axis=1, concat_axis=0, tiled=True),
    )
    query_block = query_block.reshape(block_rows, local_heads, HD)
    tail_keys, tail_values = from_behind(
        (key_block[reach_rows:], value_block[reach_rows:]), "dp", 1
    )
    starts = segment_starts(seq_lengths, key_pos)
    mixed = attend(
        query_block,
        key_block,
        value_block,
        tail_keys,
        tail_values,
        key_pos,
        key_pos,
        tail_pos,
        starts,
        reach_rows,
    )
    mixed = mixed.reshape(block_rows, 1, local_heads * HD)
    returned = lax.all_to_all(mixed, "seq", split_axis=0, concat_axis=1, tiled=True)
    return returned.reshape(tok_rows, QH * HD)


def solution(mesh):
    return jax.shard_map(
        body,
        mesh=mesh,
        in_specs=(P(("dp", "seq"), None), P(("dp", "seq"), None), P(("dp", "seq"), None), P()),
        out_specs=P(("dp", "seq"), None),
        check_vma=False,
    )
```

profile of v0, /device:TPU:4, one launch (start us, length us, event | category | flops | bytes accessed | tf_op | source)
XLA Modules:
  0.0 136.4 jit_solution(15620430314450670122)
XLA Ops:
  0.0 1.7 %copy.50 = bf16[128,512]{0,1:T(8,128)(2,1)} copy(bf16[128,512]{1,0:T(8,128)(2,1)} %param.11) | data formatting | bytes 262144 | tf_op args[1]
  1.7 4.9 %all-to-all-start.1 = ((bf16[128,4,128]{0,2,1:T(8,128)(2,1)}), bf16[128,4,128]{0,2,1:T(8,128)(2,1)S(1)}, u32[]{:S(2)}, u32[]{:S(2)}) async-start(bf16[128,4,128]{0,2,1:T(8,128)(2,1)} %bitcast.5), calls=%async_computation.1 | async-start | bytes 262144 | tf_op jit(solution)/shard_map/all_to_all | solution.py:135
  6.5 1.7 %copy.54 = bf16[128,512]{0,1:T(8,128)(2,1)} copy(bf16[128,512]{1,0:T(8,128)(2,1)} %param.12) | data formatting | bytes 262144 | tf_op args[2]
  8.2 4.4 %all-to-all-done.1 = bf16[128,4,128]{0,2,1:T(8,128)(2,1)S(1)} async-done(((bf16[128,4,128]{0,2,1:T(8,128)(2,1)}), bf16[128,4,128]{0,2,1:T(8,128)(2,1)S(1)}, u32[]{:S(2)}, u32[]{:S(2)}) %all-to-all-start.1) | async-done | bytes 131104 | tf_op jit(solution)/shard_map/all_to_all | solution.py:135
  12.6 3.3 %all-to-all-start.2 = ((bf16[128,4,128]{0,2,1:T(8,128)(2,1)}), bf16[128,4,128]{0,2,1:T(8,128)(2,1)S(1)}, u32[]{:S(2)}, u32[]{:S(2)}) async-start(bf16[128,4,128]{0,2,1:T(8,128)(2,1)} %bitcast.12), calls=%async_computation.2 | async-start | bytes 262144 | tf_op jit(solution)/shard_map/all_to_all | solution.py:136
  16.0 2.3 %copy.70 = bf16[16,4,8,1024]{3,2,0,1:T(8,128)(2,1)} copy(bf16[16,4,8,1024]{3,2,1,0:T(8,128)(2,1)} %bitcast.80) | data formatting | bytes 2097152 | tf_op jit(solution)/shard_map/reshape | solution.py:127
  18.3 3.6 %all-to-all-done.2 = bf16[128,4,128]{0,2,1:T(8,128)(2,1)S(1)} async-done(((bf16[128,4,128]{0,2,1:T(8,128)(2,1)}), bf16[128,4,128]{0,2,1:T(8,128)(2,1)S(1)}, u32[]{:S(2)}, u32[]{:S(2)}) %all-to-all-start.2) | async-done | bytes 131104 | tf_op jit(solution)/shard_map/all_to_all | solution.py:136
  21.8 3.5 %all-to-all-start = ((bf16[128,4,1024]{2,0,1:T(8,128)(2,1)}), bf16[128,4,1024]{2,0,1:T(8,128)(2,1)S(1)}, u32[]{:S(2)}, u32[]{:S(2)}) async-start(bf16[128,4,1024]{2,0,1:T(8,128)(2,1)} %bitcast.58), calls=%async_computation | async-start | bytes 2097152 | tf_op jit(solution)/shard_map/all_to_all | solution.py:134
  25.9 1.9 %collective-permute-start = (bf16[256,1,128]{2,0,1:T(8,128)(2,1)S(1)}, bf16[256,1,128]{2,0,1:T(8,128)(2,1)S(1)}, u32[]{:S(2)}, u32[]{:S(2)}) collective-permute-start(bf16[256,1,128]{2,0,1:T(8,128)(2,1)S(1)} %bitcast.91), channel_id=1, source_target_pairs={{0,4},{4,8},{8,12},{12,16},{16,20},{20,24},{24,28},{1,5},{5,9},{9,... | collective-permute-start | bytes 196616 | tf_op jit(solution)/shard_map/ppermute | solution.py:17
  28.0 3.5 %collective-permute-start.1 = (bf16[256,1,128]{2,0,1:T(8,128)(2,1)S(1)}, bf16[256,1,128]{2,0,1:T(8,128)(2,1)S(1)}, u32[]{:S(2)}, u32[]{:S(2)}) collective-permute-start(bf16[256,1,128]{2,0,1:T(8,128)(2,1)S(1)} %bitcast.92), channel_id=1, source_target_pairs={{0,4},{4,8},{8,12},{12,16},{16,20},{20,24},{24,28},{1,5},{5,9},{9,... | collective-permute-start | bytes 196616 | tf_op jit(solution)/shard_map/ppermute | solution.py:17
  31.5 0.9 compare_reduce_fusion
  32.6 16.2 %all-to-all-done = bf16[128,4,1024]{2,0,1:T(8,128)(2,1)S(1)} async-done(((bf16[128,4,1024]{2,0,1:T(8,128)(2,1)}), bf16[128,4,1024]{2,0,1:T(8,128)(2,1)S(1)}, u32[]{:S(2)}, u32[]{:S(2)}) %all-to-all-start) | async-done | bytes 1048608 | tf_op jit(solution)/shard_map/all_to_all | solution.py:134
  49.2 51.4 %while.12 = (s32[]{:T(128)}, bf16[8,512,128]{1,2,0:T(8,128)(2,1)}, s32[8]{0:T(128)S(1)}, bf16[512,8,128]{2,0,1:T(8,128)(2,1)S(1)}, bf16[512,1,128]{2,0,1:T(8,128...) while((s32[]{:T(128)}, bf16[8,512,128]{1,2,0:T(8,128)(2,1)}, ...), condition=%wide.region_12.13_spmd.clone.clone, body=%wide.region_3.12_spmd.clone.clone.sunk | while | flops 207420416 | bytes 8435984 | solution.py:111
  58.8 0.7 conditional.8
  65.2 0.7 conditional.8
  71.7 0.7 conditional.8
  78.1 0.7 conditional.8
  84.5 0.7 conditional.8
  90.9 0.7 conditional.8
  101.2 2.7 %reduce.1 = bf16[512,1024]{0,1:T(8,128)(2,1)S(1)} reduce(bf16[512,1,1024]{0,2,1:T(8,128)(2,1)} %bitcast.79, bf16[]{:T(256)} %broadcast.33), dimensions={1}, to_apply=%copy.59.reduce_sub_computation | reduce | bytes 2097154 | tf_op jit(solution)/shard_map/reshape | solution.py:155
  104.5 0.8 reshape.80
  105.3 27.7 %all_to_all.66 = bf16[4,2,65536]{2,1,0:T(2,128)(2,1)S(1)} all-to-all(bf16[4,2,65536]{2,1,0:T(2,128)(2,1)S(1)} %reshape.80), channel_id=1, replica_groups=mesh['dp'=8,'seq'=4] {'seq'}, dimensions={0} | all-to-all | bytes 2097152 | tf_op jit(solution)/shard_map/all_to_all | solution.py:156
  133.0 0.9 reshape.81
  135.0 1.3 copy.61
  (155 shorter events, 38.1 us)
Async XLA Ops:
  1.7 10.9 %all-to-all-start.1 = ((bf16[128,4,128]{0,2,1:T(8,128)(2,1)}), bf16[128,4,128]{0,2,1:T(8,128)(2,1)S(1)}, u32[]{:S(2)}, u32[]{:S(2)}) async-start(bf16[128,4,128]{0,2,1:T(8,128)(2,1)} %bitcast.5), calls=%async_computation.1 | async-start | bytes 262144 | tf_op jit(solution)/shard_map/all_to_all | solution.py:135
  12.6 9.2 %all-to-all-start.2 = ((bf16[128,4,128]{0,2,1:T(8,128)(2,1)}), bf16[128,4,128]{0,2,1:T(8,128)(2,1)S(1)}, u32[]{:S(2)}, u32[]{:S(2)}) async-start(bf16[128,4,128]{0,2,1:T(8,128)(2,1)} %bitcast.12), calls=%async_computation.2 | async-start | bytes 262144 | tf_op jit(solution)/shard_map/all_to_all | solution.py:136
  15.9 9.4 %copy-start = (s32[32]{0:T(128)S(1)}, s32[32]{0:T(128)}, u32[]{:S(2)}) copy-start(s32[32]{0:T(128)} %param.13) | copy-start | bytes 388
  21.8 27.0 %all-to-all-start = ((bf16[128,4,1024]{2,0,1:T(8,128)(2,1)}), bf16[128,4,1024]{2,0,1:T(8,128)(2,1)S(1)}, u32[]{:S(2)}, u32[]{:S(2)}) async-start(bf16[128,4,1024]{2,0,1:T(8,128)(2,1)} %bitcast.58), calls=%async_computation | async-start | bytes 2097152 | tf_op jit(solution)/shard_map/all_to_all | solution.py:134
  25.9 23.3 %collective-permute-start = (bf16[256,1,128]{2,0,1:T(8,128)(2,1)S(1)}, bf16[256,1,128]{2,0,1:T(8,128)(2,1)S(1)}, u32[]{:S(2)}, u32[]{:S(2)}) collective-permute-start(bf16[256,1,128]{2,0,1:T(8,128)(2,1)S(1)} %bitcast.91), channel_id=1, source_target_pairs={{0,4},{4,8},{8,12},{12,16},{16,20},{20,24},{24,28},{1,5},{5,9},{9,... | collective-permute-start | bytes 196616 | tf_op jit(solution)/shard_map/ppermute | solution.py:17
  28.0 21.3 %collective-permute-start.1 = (bf16[256,1,128]{2,0,1:T(8,128)(2,1)S(1)}, bf16[256,1,128]{2,0,1:T(8,128)(2,1)S(1)}, u32[]{:S(2)}, u32[]{:S(2)}) collective-permute-start(bf16[256,1,128]{2,0,1:T(8,128)(2,1)S(1)} %bitcast.92), channel_id=1, source_target_pairs={{0,4},{4,8},{8,12},{12,16},{16,20},{20,24},{24,28},{1,5},{5,9},{9,... | collective-permute-start | bytes 196616 | tf_op jit(solution)/shard_map/ppermute | solution.py:17
where the time goes:
time: 137 us; the launch traced here: 136 us
  blocking collectives  27.7 us (20%)
  local copies, waits for them, and re-layouts  26.2 us (19%)
  waiting for transfers between devices  24.2 us (18%)
  loops' own time  20 us (15%)
  starting transfers between devices  17.1 us (12%)
  matrix products  10.9 us (8%)
  other arithmetic  10 us (7%)
    all_to_all x1, blocking collectives, body(): lax.all_to_all(mixed, 'seq', split_axis=0, concat_axis=1, tiled=True)  27.7 us
    another operation x1, loops' own time, attend(): per_head = lax.map(one_head, jnp.arange(heads_query, dtype=jnp.int32))  19.6 us
    all_to_all x1, waiting for transfers between devices, body(): lax.all_to_all(query_split, 'seq', split_axis=1, concat_axis=0, tiled=True)  16.2 us
    unnamed x10, local copies, waits for them, and re-layouts  6.39 us
    dynamic_update_slice x16, local copies, waits for them, and re-layouts, attend(): per_head = lax.map(one_head, jnp.arange(heads_query, dtype=jnp.int32))  6.27 us
    ppermute x2, starting transfers between devices, from_behind(): return lax.ppermute(block, axis, route)  5.42 us
    all_to_all x1, starting transfers between devices, body(): lax.all_to_all(key_split, 'seq', split_axis=1, concat_axis=0, tiled=True)  4.87 us
    dynamic_slice x8, local copies, waits for them, and re-layouts, attend(): per_head = lax.map(one_head, jnp.arange(heads_query, dtype=jnp.int32))  4.64 us
  transfers between devices with their start and end apart: 5, of which 3 were waited for; matrix products, arithmetic and copies ran while one was open for 4% of the time, Pallas kernels for 0%

commit v1 on v0

--- a/solution.py
+++ b/solution.py
@@ -153,7 +153,10 @@
         reach_rows,
     )
     mixed = mixed.reshape(block_rows, 1, local_heads * HD)
-    returned = lax.all_to_all(mixed, "seq", split_axis=0, concat_axis=1, tiled=True)
+    returned = jnp.concatenate(
+        lax.all_to_all(jnp.stack(jnp.split(mixed, lax.axis_size("seq"), axis=0)), "seq", 0, 0),
+        axis=1,
+    )
     return returned.reshape(tok_rows, QH * HD)
 
 

time: 137 us -> 132 us (0.964)
  local copies, waits for them, and re-layouts: 26.2 us -> 23 us
  other arithmetic: 10 us -> 7.45 us
    reshape x1 -> x0, other arithmetic: 2.72 us -> none  [body(): mixed = mixed.reshape(block_rows, 1, local_heads * HD)]
    unnamed x10 -> x8, local copies, waits for them, and re-layouts: 6.39 us -> 4.47 us
    reshape x2 -> x0, local copies, waits for them, and re-layouts: 1.9 us -> none  [the longest x1 1.31 us: body(): return returned.reshape(tok_rows, QH * HD)]
    another operation x9 -> x10, local copies, waits for them, and re-layouts: 1.78 us -> 3.08 us
where the time goes in v1:
time: 132 us; the launch traced here: 131 us
  blocking collectives  27.7 us (21%)
  waiting for transfers between devices  24.7 us (19%)
  local copies, waits for them, and re-layouts  23 us (17%)
  loops' own time  20 us (15%)
  starting transfers between devices  17.1 us (13%)
  matrix products  10.9 us (8%)
  other arithmetic  7.45 us (6%)
    all_to_all x1, blocking collectives, body(): lax.all_to_all(jnp.stack(jnp.split(mixed, lax.axis_size('seq'), axis=0)),...  27.7 us
    another operation x1, loops' own time, attend(): per_head = lax.map(one_head, jnp.arange(heads_query, dtype=jnp.int32))  19.6 us
    all_to_all x1, waiting for transfers between devices, body(): lax.all_to_all(query_split, 'seq', split_axis=1, concat_axis=0, tiled=True)  15.5 us
    dynamic_update_slice x16, local copies, waits for them, and re-layouts, attend(): per_head = lax.map(one_head, jnp.arange(heads_query, dtype=jnp.int32))  6.27 us
    ppermute x2, starting transfers between devices, from_behind(): return lax.ppermute(block, axis, route)  5.42 us
    all_to_all x1, starting transfers between devices, body(): lax.all_to_all(key_split, 'seq', split_axis=1, concat_axis=0, tiled=True)  4.87 us
    all_to_all x1, waiting for transfers between devices, body(): lax.all_to_all(value_split, 'seq', split_axis=1, concat_axis=0, tiled=True)  4.8 us
    dynamic_slice x8, local copies, waits for them, and re-layouts, attend(): per_head = lax.map(one_head, jnp.arange(heads_query, dtype=jnp.int32))  4.64 us
  transfers between devices with their start and end apart: 5, of which 3 were waited for; matrix products, arithmetic and copies ran while one was open for 4% of the time, Pallas kernels for 0%

profile of v1, /device:TPU:4, one launch (start us, length us, event | category | flops | bytes accessed | tf_op | source)
XLA Modules:
  0.0 131.2 jit_solution(17276034941773805597)
XLA Ops:
  0.0 1.8 %copy.33 = bf16[128,512]{0,1:T(8,128)(2,1)} copy(bf16[128,512]{1,0:T(8,128)(2,1)} %param.11) | data formatting | bytes 262144 | tf_op args[1]
  1.8 4.9 %all-to-all-start.1 = ((bf16[128,4,128]{0,2,1:T(8,128)(2,1)}), bf16[128,4,128]{0,2,1:T(8,128)(2,1)S(1)}, u32[]{:S(2)}, u32[]{:S(2)}) async-start(bf16[128,4,128]{0,2,1:T(8,128)(2,1)} %bitcast.5), calls=%async_computation.1 | async-start | bytes 262144 | tf_op jit(solution)/shard_map/all_to_all | solution.py:135
  6.6 1.7 %copy.37 = bf16[128,512]{0,1:T(8,128)(2,1)} copy(bf16[128,512]{1,0:T(8,128)(2,1)} %param.12) | data formatting | bytes 262144 | tf_op args[2]
  8.3 4.4 %all-to-all-done.1 = bf16[128,4,128]{0,2,1:T(8,128)(2,1)S(1)} async-done(((bf16[128,4,128]{0,2,1:T(8,128)(2,1)}), bf16[128,4,128]{0,2,1:T(8,128)(2,1)S(1)}, u32[]{:S(2)}, u32[]{:S(2)}) %all-to-all-start.1) | async-done | bytes 131104 | tf_op jit(solution)/shard_map/all_to_all | solution.py:135
  12.7 3.3 %all-to-all-start.2 = ((bf16[128,4,128]{0,2,1:T(8,128)(2,1)}), bf16[128,4,128]{0,2,1:T(8,128)(2,1)S(1)}, u32[]{:S(2)}, u32[]{:S(2)}) async-start(bf16[128,4,128]{0,2,1:T(8,128)(2,1)} %bitcast.12), calls=%async_computation.2 | async-start | bytes 262144 | tf_op jit(solution)/shard_map/all_to_all | solution.py:136
  16.0 1.1 copy.50
  17.1 4.8 %all-to-all-done.2 = bf16[128,4,128]{0,2,1:T(8,128)(2,1)S(1)} async-done(((bf16[128,4,128]{0,2,1:T(8,128)(2,1)}), bf16[128,4,128]{0,2,1:T(8,128)(2,1)S(1)}, u32[]{:S(2)}, u32[]{:S(2)}) %all-to-all-start.2) | async-done | bytes 131104 | tf_op jit(solution)/shard_map/all_to_all | solution.py:136
  21.9 3.5 %all-to-all-start = ((bf16[128,4,1024]{2,0,1:T(8,128)(2,1)}), bf16[128,4,1024]{2,0,1:T(8,128)(2,1)S(1)}, u32[]{:S(2)}, u32[]{:S(2)}) async-start(bf16[128,4,1024]{2,0,1:T(8,128)(2,1)} %bitcast.59), calls=%async_computation | async-start | bytes 2097152 | tf_op jit(solution)/shard_map/all_to_all | solution.py:134
  26.6 1.9 %collective-permute-start = (bf16[256,1,128]{2,0,1:T(8,128)(2,1)S(1)}, bf16[256,1,128]{2,0,1:T(8,128)(2,1)S(1)}, u32[]{:S(2)}, u32[]{:S(2)}) collective-permute-start(bf16[256,1,128]{2,0,1:T(8,128)(2,1)S(1)} %bitcast.95), channel_id=1, source_target_pairs={{0,4},{4,8},{8,12},{12,16},{16,20},{20,24},{24,28},{1,5},{5,9},{9,... | collective-permute-start | bytes 196616 | tf_op jit(solution)/shard_map/ppermute | solution.py:17
  28.7 3.5 %collective-permute-start.1 = (bf16[256,1,128]{2,0,1:T(8,128)(2,1)S(1)}, bf16[256,1,128]{2,0,1:T(8,128)(2,1)S(1)}, u32[]{:S(2)}, u32[]{:S(2)}) collective-permute-start(bf16[256,1,128]{2,0,1:T(8,128)(2,1)S(1)} %bitcast.96), channel_id=1, source_target_pairs={{0,4},{4,8},{8,12},{12,16},{16,20},{20,24},{24,28},{1,5},{5,9},{9,... | collective-permute-start | bytes 196616 | tf_op jit(solution)/shard_map/ppermute | solution.py:17
  32.2 0.9 compare_reduce_fusion
  33.4 15.5 %all-to-all-done = bf16[128,4,1024]{2,0,1:T(8,128)(2,1)S(1)} async-done(((bf16[128,4,1024]{2,0,1:T(8,128)(2,1)}), bf16[128,4,1024]{2,0,1:T(8,128)(2,1)S(1)}, u32[]{:S(2)}, u32[]{:S(2)}) %all-to-all-start) | async-done | bytes 1048608 | tf_op jit(solution)/shard_map/all_to_all | solution.py:134
  49.3 51.4 %while.12 = (s32[]{:T(128)}, bf16[8,512,128]{1,2,0:T(8,128)(2,1)}, s32[8]{0:T(128)S(1)}, bf16[512,8,128]{2,0,1:T(8,128)(2,1)S(1)}, bf16[512,1,128]{2,0,1:T(8,128...) while((s32[]{:T(128)}, bf16[8,512,128]{1,2,0:T(8,128)(2,1)}, ...), condition=%wide.region_12.13_spmd.clone.clone, body=%wide.region_3.12_spmd.clone.clone.sunk | while | flops 207420416 | bytes 8435984 | solution.py:111
  52.5 0.7 conditional.8
  58.9 0.7 conditional.8
  65.3 0.7 conditional.8
  71.8 0.7 conditional.8
  78.2 0.7 conditional.8
  84.6 0.7 conditional.8
  91.0 0.7 conditional.8
  97.5 0.7 conditional.8
  100.7 1.3 fusion.27
  102.2 27.7 %all_to_all.56 = bf16[4,128,1,1024]{1,3,2,0:T(8,128)(2,1)S(1)} all-to-all(bf16[4,128,1,1024]{1,3,2,0:T(8,128)(2,1)S(1)} %pad_maximum_fusion), channel_id=1, replica_groups=mesh['dp'=8,'seq'=4] {'seq'}, dimensions={0} | all-to-all | bytes 2097152 | tf_op jit(solution)/shard_map/all_to_all | solution.py:157
  129.9 1.3 copy.42
  (152 shorter events, 35.3 us)
Async XLA Ops:
  0.0 16.0 %copy-start = (bf16[128,4096]{1,0:T(8,128)(2,1)S(1)}, bf16[128,4096]{1,0:T(8,128)(2,1)}, u32[]{:S(2)}) copy-start(bf16[128,4096]{1,0:T(8,128)(2,1)} %param.10) | copy-start | bytes 3145732
  1.8 10.9 %all-to-all-start.1 = ((bf16[128,4,128]{0,2,1:T(8,128)(2,1)}), bf16[128,4,128]{0,2,1:T(8,128)(2,1)S(1)}, u32[]{:S(2)}, u32[]{:S(2)}) async-start(bf16[128,4,128]{0,2,1:T(8,128)(2,1)} %bitcast.5), calls=%async_computation.1 | async-start | bytes 262144 | tf_op jit(solution)/shard_map/all_to_all | solution.py:135
  12.7 9.2 %all-to-all-start.2 = ((bf16[128,4,128]{0,2,1:T(8,128)(2,1)}), bf16[128,4,128]{0,2,1:T(8,128)(2,1)S(1)}, u32[]{:S(2)}, u32[]{:S(2)}) async-start(bf16[128,4,128]{0,2,1:T(8,128)(2,1)} %bitcast.12), calls=%async_computation.2 | async-start | bytes 262144 | tf_op jit(solution)/shard_map/all_to_all | solution.py:136
  21.9 27.0 %all-to-all-start = ((bf16[128,4,1024]{2,0,1:T(8,128)(2,1)}), bf16[128,4,1024]{2,0,1:T(8,128)(2,1)S(1)}, u32[]{:S(2)}, u32[]{:S(2)}) async-start(bf16[128,4,1024]{2,0,1:T(8,128)(2,1)} %bitcast.59), calls=%async_computation | async-start | bytes 2097152 | tf_op jit(solution)/shard_map/all_to_all | solution.py:134
  25.5 0.7 copy-start.1
  26.6 22.7 %collective-permute-start = (bf16[256,1,128]{2,0,1:T(8,128)(2,1)S(1)}, bf16[256,1,128]{2,0,1:T(8,128)(2,1)S(1)}, u32[]{:S(2)}, u32[]{:S(2)}) collective-permute-start(bf16[256,1,128]{2,0,1:T(8,128)(2,1)S(1)} %bitcast.95), channel_id=1, source_target_pairs={{0,4},{4,8},{8,12},{12,16},{16,20},{20,24},{24,28},{1,5},{5,9},{9,... | collective-permute-start | bytes 196616 | tf_op jit(solution)/shard_map/ppermute | solution.py:17
  28.7 20.6 %collective-permute-start.1 = (bf16[256,1,128]{2,0,1:T(8,128)(2,1)S(1)}, bf16[256,1,128]{2,0,1:T(8,128)(2,1)S(1)}, u32[]{:S(2)}, u32[]{:S(2)}) collective-permute-start(bf16[256,1,128]{2,0,1:T(8,128)(2,1)S(1)} %bitcast.96), channel_id=1, source_target_pairs={{0,4},{4,8},{8,12},{12,16},{16,20},{20,24},{24,28},{1,5},{5,9},{9,... | collective-permute-start | bytes 196616 | tf_op jit(solution)/shard_map/ppermute | solution.py:17
